TPU v7x, 256 devices: a whole 4x4x8 slice. The times are simulated.
256 devices in a mesh: row: 16 (over z, y_hi), col: 16 (over y_lo, x, core).
Axes of the slice: x: 4, y: 4 (y_hi: 2, y_lo: 2; y = y_hi * 2 + y_lo), z: 8, core: 2. Of those that a mesh axis runs over, the one named last changes fastest.
Arguments:
- amplitudes: bfloat16 [2048, 32768], P('row', 'col'), may hold values from -6 to 6
- amp_mask: int32 [64, 128], P('row', 'col'), may hold values from 0 to 1, as said below
- integrals: bfloat16 [16384, 32768], P('row', 'col'), may hold values from -0.0625 to 0.0625
- int_mask: int32 [64, 128], P('row', 'col'), may hold values 0 or 1
- occ_energy: float32 [2048], P('col'), may hold values from -1.5 to -0.5
- vir_energy: float32 [16384], P('row'), may hold values from 0.5 to 1.5
Outputs:
- residual: bfloat16 [2048, 16384], P('col', 'row')
Inputs may be any that keep to these rules, and one draw needn't show every extreme that they name: In every row of amp_mask, each aligned group of 8 consecutive entries holds exactly 4 ones.
All inputs are finite; a program needn't handle non-finite values. No bound on the sum of `int_mask` on one device may be relied on, other than what follows from the above.
Results may differ from a plain program's by a relative error of at most 0.001.
Values may be sent and summed in bfloat16 or wider, within the bound.
A program may use at most 64 MiB of HBM per device.

v0:
```python
import jax
import jax.numpy as jnp
from jax import lax
from jax.sharding import PartitionSpec as P

TILE = 256
IJ_BLK = 32


def expand_tiles(values, keep, rows_tile, cols_tile):
    nrow, ncol = keep.shape
    shaped = values.reshape(nrow, rows_tile, ncol, cols_tile)
    return (shaped * keep.astype(values.dtype)[:, None, :, None]).reshape(values.shape)


def contract(left, right):
    return lax.dot_general(
        left, right, (((1,), (1,)), ((), ())), preferred_element_type=jnp.float32
    )


def whole_sum(partial_value):
    return lax.psum_scatter(partial_value, "col", scatter_dimension=0, tiled=True)


def body(amplitudes, amp_mask, integrals, int_mask, occ_energy, vir_energy):
    int_used = expand_tiles(integrals, int_mask, TILE, TILE)
    amp_used = expand_tiles(amplitudes, amp_mask, IJ_BLK, TILE)
    partial_value = contract(lax.all_gather(amp_used, "row", axis=0, tiled=True), int_used)
    ladder = whole_sum(partial_value)
    denom = vir_energy[None, :] - occ_energy[:, None]
    return (ladder / denom).astype(jnp.bfloat16)


def solution(mesh):
    return jax.shard_map(
        body,
        mesh=mesh,
        in_specs=(
            P("row", "col"),
            P("row", "col"),
            P("row", "col"),
            P("row", "col"),
            P("col"),
            P("row"),
        ),
        out_specs=P("col", "row"),
        check_vma=False,
    )
```

profile of v0, /device:TPU:32, one launch (start us, length us, event | category | flops | bytes accessed | tf_op | source)
XLA Modules:
  0.0 246.6 jit_solution(13339371365637120035)
XLA Ops:
  6.5 0.0 all-gather.2.cloned.1.call-start
  6.5 0.7 convert_element_type.9
  7.2 0.1 mul.22
  7.3 0.1 copy.7
  7.5 2.0 mul.24
  9.5 0.0 all-gather.2.cloned.1.call-update
  9.5 0.0 reduce-scatter.2.cloned.1.call-start
  9.5 0.7 convert_element_type.10
  10.2 0.3 mul.25
  10.6 3.4 %copy.8 = bf16[128,8,8,256]{3,1,2,0:T(8,128)(2,1)} copy(bf16[128,8,8,256]{3,2,1,0:T(8,128)(2,1)S(1)} %bitcast.7) | data formatting | bytes 8388608
  14.0 132.0 %all-gather.2.cloned.1.call-done = bf16[2048,2048]{1,0:T(8,128)(2,1)} async-done(((bf16[128,2048]{1,0:T(8,128)(2,1)}), bf16[2048,2048]{1,0:T(8,128)(2,1)}) %all-gather.2.cloned.1.call-update) | async-done | bytes 8388624 | tf_op jit(solution)/shard_map/all_gather | solution.py:29
  146.0 15.8 %fusion = f32[2048,1024]{1,0:T(8,128)} fusion(bf16[2048,2048]{1,0:T(8,128)(2,1)} %all-gather.2.cloned.1.call-done, bf16[1024,2048]{1,0:T(8,128)(2,1)} %param.8, bf16[1024,2048]{1,0:T(8,128)(2,1)} %bitcast.8), kind=kOutput, calls=%fused_computation | convolution fusion | flops 8592031744 | bytes 25165824 | tf_op jit(solution)/shard_map/dot_general | solution.py:17
  161.8 0.0 copy-start
  161.8 0.0 copy-start.1
  161.8 0.0 reduce-scatter.2.cloned.1.call-update
  161.8 76.1 %reduce-scatter.2.cloned.1.call-done = f32[128,1024]{1,0:T(8,128)} async-done(((f32[2048,1024]{1,0:T(8,128)}), f32[128,1024]{1,0:T(8,128)}) %reduce-scatter.2.cloned.1.call-update) | async-done | bytes 524304 | tf_op jit(solution)/shard_map/reduce_scatter | solution.py:23
  237.9 0.0 copy-done
  237.9 0.0 copy-done.1
  237.9 1.9 divide_convert_fusion
Async XLA Ops:
  6.5 139.5 %all-gather.2.cloned.1.call-start = ((), (), s32[]{:S(2)}) async-start(), calls=%async_computation.1 | async-start | bytes 8912896 | tf_op jit(solution)/shard_map/all_gather | solution.py:29
  9.5 228.4 %reduce-scatter.2.cloned.1.call-start = ((), (), s32[]{:S(2)}) async-start(), calls=%async_computation.2 | async-start | bytes 8912896 | tf_op jit(solution)/shard_map/reduce_scatter | solution.py:23
  161.8 76.1 %copy-start = (f32[1024]{0:T(1024)S(1)}, f32[1024]{0:T(1024)}, u32[]{:S(2)}) copy-start(f32[1024]{0:T(1024)} %param.11) | copy-start | bytes 12292
  161.8 76.1 %copy-start.1 = (f32[128]{0:T(128)S(1)}, f32[128]{0:T(128)}, u32[]{:S(2)}) copy-start(f32[128]{0:T(128)} %param.10) | copy-start | bytes 1540
Sparse Core Ops, SparseCore 0:
  9.9 136.0 all-gather.1
  162.0 75.8 reduce-scatter.1
where the time goes:
time: 247 us
  waiting for transfers between devices  208 us (84%)
  matrix products  15.8 us (6%)
  between operations  13.4 us (5%)
  other arithmetic  5.27 us (2%)
  local copies, waits for them, and re-layouts  3.96 us (2%)
    all_gather x1, waiting for transfers between devices, body(): lax.all_gather(amp_used, 'row', axis=0, tiled=True)  132 us
    reduce_scatter x1, waiting for transfers between devices, whole_sum(): lax.psum_scatter(partial_value, 'col', scatter_dimension=0, tiled=True)  76.1 us
    dot_general x1, matrix products, contract(): lax.dot_general(left, right, (((1,), (1,)), ((), ())), preferred_element_...  15.8 us
  transfers between devices with their start and end apart: 2, of which 2 were waited for; matrix products, arithmetic and copies ran while one was open for 2% of the time, Pallas kernels for 0%

commit v1 on v0

--- a/solution.py
+++ b/solution.py
@@ -5,6 +5,11 @@
 
 TILE = 256
 IJ_BLK = 32
+
+
+def exchange_gather(array, axis, along):
+    stack = jnp.stack([array] * lax.axis_size(axis))
+    return jnp.concatenate(lax.all_to_all(stack, axis, 0, 0), axis=along)
 
 
 def expand_tiles(values, keep, rows_tile, cols_tile):
@@ -26,7 +31,7 @@
 def body(amplitudes, amp_mask, integrals, int_mask, occ_energy, vir_energy):
     int_used = expand_tiles(integrals, int_mask, TILE, TILE)
     amp_used = expand_tiles(amplitudes, amp_mask, IJ_BLK, TILE)
-    partial_value = contract(lax.all_gather(amp_used, "row", axis=0, tiled=True), int_used)
+    partial_value = contract(exchange_gather(amp_used, "row", 0), int_used)
     ladder = whole_sum(partial_value)
     denom = vir_energy[None, :] - occ_energy[:, None]
     return (ladder / denom).astype(jnp.bfloat16)

time: 247 us -> 318 us (1.29)
  waiting for transfers between devices: 208 us -> 266 us
  starting transfers between devices: 0.04 us -> 11.4 us
  local copies, waits for them, and re-layouts: 3.96 us -> 8.25 us
    all_to_all x0 -> x1, waiting for transfers between devices: none -> 189 us  [exchange_gather(): return jnp.concatenate(lax.all_to_all(stack, axis, 0, 0), axis=along)]
    all_gather x1 -> x0, waiting for transfers between devices: 132 us -> none  [body(): lax.all_gather(amp_used, 'row', axis=0, tiled=True)]
    all_to_all x0 -> x1, starting transfers between devices: none -> 11.3 us  [exchange_gather(): return jnp.concatenate(lax.all_to_all(stack, axis, 0, 0), axis=along)]
    another operation x0 -> x1, local copies, waits for them, and re-layouts: none -> 4.28 us  [exchange_gather(): stack = jnp.stack([array] * lax.axis_size(axis))]
  transfers between devices with their start and end apart: 2 -> 2, of which waited for: 2 -> 2; matrix products, arithmetic and copies ran while one was open for 2% -> 1% of each run, Pallas kernels for 0% -> 0%
where the time goes in v1:
time: 318 us
  waiting for transfers between devices  266 us (84%)
  matrix products  15.8 us (5%)
  between operations  13.4 us (4%)
  starting transfers between devices  11.4 us (4%)
  local copies, waits for them, and re-layouts  8.25 us (3%)
  other arithmetic  3.75 us (1%)
    all_to_all x1, waiting for transfers between devices, exchange_gather(): return jnp.concatenate(lax.all_to_all(stack, axis, 0, 0), axis=along)  189 us
    reduce_scatter x1, waiting for transfers between devices, whole_sum(): lax.psum_scatter(partial_value, 'col', scatter_dimension=0, tiled=True)  76.8 us
    dot_general x1, matrix products, contract(): lax.dot_general(left, right, (((1,), (1,)), ((), ())), preferred_element_...  15.8 us
    all_to_all x1, starting transfers between devices, exchange_gather(): return jnp.concatenate(lax.all_to_all(stack, axis, 0, 0), axis=along)  11.3 us
  transfers between devices with their start and end apart: 2, of which 2 were waited for; matrix products, arithmetic and copies ran while one was open for 1% of the time, Pallas kernels for 0%

profile of v1, /device:TPU:32, one launch (start us, length us, event | category | flops | bytes accessed | tf_op | source)
XLA Modules:
  0.0 318.2 jit_solution(4140144668496321058)
XLA Ops:
  6.5 0.7 convert_element_type.9
  7.2 0.1 mul.23
  7.3 0.1 copy.7
  7.4 1.2 mul.25
  8.6 4.3 %stack.3 = bf16[16,128,2048]{2,1,0:T(8,128)(2,1)} broadcast(bf16[128,2048]{1,0:T(8,128)(2,1)S(1)} %mul.25), dimensions={1,2} | broadcast | bytes 8912896 | tf_op jit(solution)/shard_map/stack | solution.py:11
  12.9 0.0 copy-start.1
  12.9 11.3 %all-to-all-start = ((bf16[16,128,2048]{2,1,0:T(8,128)(2,1)}), bf16[16,128,2048]{2,1,0:T(8,128)(2,1)}, u32[]{:S(2)}, u32[]{:S(2)}) async-start(bf16[16,128,2048]{2,1,0:T(8,128)(2,1)} %stack.3), calls=%async_computation | async-start | bytes 16777216 | tf_op jit(solution)/shard_map/all_to_all | solution.py:12
  24.3 0.0 reduce-scatter.2.cloned.1.call-start
  24.3 0.0 copy-done.1
  24.3 0.3 mul.26
  24.7 3.4 %copy.8 = bf16[128,8,8,256]{3,1,2,0:T(8,128)(2,1)} copy(bf16[128,8,8,256]{3,2,1,0:T(8,128)(2,1)S(1)} %bitcast.8) | data formatting | bytes 8388608
  28.1 188.7 %all-to-all-done = bf16[16,128,2048]{2,1,0:T(8,128)(2,1)} async-done(((bf16[16,128,2048]{2,1,0:T(8,128)(2,1)}), bf16[16,128,2048]{2,1,0:T(8,128)(2,1)}, u32[]{:S(2)}, u32[]{:S(2)}) %all-to-all-start) | async-done | bytes 8388640 | tf_op jit(solution)/shard_map/all_to_all | solution.py:12
  216.8 15.8 %fusion = f32[2048,1024]{1,0:T(8,128)} fusion(bf16[2048,2048]{1,0:T(8,128)(2,1)} %bitcast, bf16[1024,2048]{1,0:T(8,128)(2,1)} %param.8, bf16[1024,2048]{1,0:T(8,128)(2,1)} %bitcast.9), kind=kOutput, calls=%fused_computation | convolution fusion | flops 8592031744 | bytes 25165824 | tf_op jit(solution)/shard_map/dot_general | solution.py:22
  232.6 0.0 copy-start
  232.6 0.0 copy-start.2
  232.6 0.0 reduce-scatter.2.cloned.1.call-update
  232.6 76.8 %reduce-scatter.2.cloned.1.call-done = f32[128,1024]{1,0:T(8,128)} async-done(((f32[2048,1024]{1,0:T(8,128)}), f32[128,1024]{1,0:T(8,128)}) %reduce-scatter.2.cloned.1.call-update) | async-done | bytes 524304 | tf_op jit(solution)/shard_map/reduce_scatter | solution.py:28
  309.4 0.0 copy-done
  309.4 0.0 copy-done.2
  309.4 1.9 divide_convert_fusion
  (1 shorter events, 0.0 us)
Async XLA Ops:
  12.9 11.4 %copy-start.1 = (s32[4,8]{1,0:T(4,128)S(1)}, s32[4,8]{1,0:T(4,128)}, u32[]{:S(2)}) copy-start(s32[4,8]{1,0:T(4,128)} %param.9) | copy-start | bytes 388
  12.9 203.9 %all-to-all-start = ((bf16[16,128,2048]{2,1,0:T(8,128)(2,1)}), bf16[16,128,2048]{2,1,0:T(8,128)(2,1)}, u32[]{:S(2)}, u32[]{:S(2)}) async-start(bf16[16,128,2048]{2,1,0:T(8,128)(2,1)} %stack.3), calls=%async_computation | async-start | bytes 16777216 | tf_op jit(solution)/shard_map/all_to_all | solution.py:12
  24.3 285.2 %reduce-scatter.2.cloned.1.call-start = ((), (), s32[]{:S(2)}) async-start(), calls=%async_computation.2 | async-start | bytes 8912896 | tf_op jit(solution)/shard_map/reduce_scatter | solution.py:28
  232.6 76.8 %copy-start = (f32[1024]{0:T(1024)S(1)}, f32[1024]{0:T(1024)}, u32[]{:S(2)}) copy-start(f32[1024]{0:T(1024)} %param.11) | copy-start | bytes 12292
  232.6 76.8 %copy-start.2 = (f32[128]{0:T(128)S(1)}, f32[128]{0:T(128)}, u32[]{:S(2)}) copy-start(f32[128]{0:T(128)} %param.10) | copy-start | bytes 1540
Sparse Core Ops, SparseCore 0:
  232.8 76.6 reduce-scatter.1
